TPU v7x, 32 devices: a whole 2x2x4 slice. The times are simulated.
32 devices in a mesh: groups: 2 (over x), tm: 8 (over z, y), space: 2 (over core).
Axes of the slice: x: 2, y: 2, z: 4, core: 2. Of those that a mesh axis runs over, the one named last changes fastest.
Arguments:
- query_pre: bfloat16 [16, 8, 32, 2240], P(('groups', 'tm'), 'space'), parts along dimension 0, may hold values from -6 to 6
- key_pre: bfloat16 [16, 8, 32, 2240], P(('groups', 'tm'), 'space'), parts along dimension 0, may hold values from -6 to 6
- value_pre: bfloat16 [16, 8, 32, 2240], P(('groups', 'tm'), 'space'), parts along dimension 0, may hold values from -8 to 8
- grad_out: bfloat16 [16, 8, 32, 2240], P(('groups', 'tm'), 'space'), parts along dimension 0, may hold values from -96 to 96
- conv_taps: float32 [3, 3, 2240], replicated, may hold values from -4 to 4
Outputs:
- attended: bfloat16 [16, 8, 32, 2240], P(('groups', 'tm'), 'space'), parts along dimension 0
- query_grad: bfloat16 [16, 8, 32, 2240], P(('groups', 'tm'), 'space'), parts along dimension 0
- key_grad: bfloat16 [16, 8, 32, 2240], P(('groups', 'tm'), 'space'), parts along dimension 0
- value_grad: bfloat16 [16, 8, 32, 2240], P(('groups', 'tm'), 'space'), parts along dimension 0
- taps_grad: float32 [6, 3, 2240], P('groups'), parts along dimension 0
There are 2 independent parts, one for each index of `groups`. A program takes and returns all parts, laid end to end along the dimension named above; an argument that names none is the same for every part. Nothing has to cross between parts.
All inputs are finite; a program needn't handle non-finite values.
Results may differ from a plain program's by a relative error of at most 0.013.
Values may be sent and summed in bfloat16 or wider, within the bound.
A program may use at most 128 MiB of HBM per device.

v0:
```python
import jax
import jax.numpy as jnp
from jax import lax
from jax.sharding import PartitionSpec as P

HEADS = 20
HEAD_DIM = 112


def extended(block, sides, width):
    for axis, dim in sides:
        count = lax.axis_size(axis)
        forward = [(i, i + 1) for i in range(count - 1)]
        backward = [(target, source) for source, target in forward]
        low = lax.ppermute(
            lax.slice_in_dim(block, block.shape[dim] - width, None, axis=dim), axis, forward
        )
        high = lax.ppermute(lax.slice_in_dim(block, 0, width, axis=dim), axis, backward)
        block = jnp.concatenate([low, block, high], axis=dim)
    return block


def carried_in(part, axis, combine, identity):
    place = lax.axis_index(axis)
    gathered = jax.tree.map(lambda a: lax.all_gather(a, axis), part)
    state = jax.tree.map(lambda a, e: jnp.zeros_like(a) + jnp.asarray(e, a.dtype), part, identity)

    def one(turn, state):
        return combine(
            state, jax.tree.map(lambda a: lax.dynamic_index_in_dim(a, turn, 0, False), gathered)
        )

    return lax.fori_loop(0, place, one, state)


def carried_in_2(x, axis, join, neutral):
    count = lax.axis_size(axis)
    place = lax.axis_index(axis)
    ahead = count - 1 - place
    gathered = jax.tree.map(
        lambda a, kind: lax.all_gather(a.astype(kind), axis), x, (jnp.bfloat16, jnp.bfloat16)
    )
    state = jax.tree.map(lambda a, e: jnp.zeros_like(a) + jnp.asarray(e, a.dtype), x, neutral)

    def one(turn, state):
        source = count - 1 - turn
        return join(
            state,
            jax.tree.map(
                lambda a, own: lax.dynamic_index_in_dim(a, source, 0, False).astype(own.dtype),
                gathered,
                x,
            ),
        )

    return lax.fori_loop(0, ahead, one, state)


def mix_rows(padded, conv_taps, row_count, col_count, flipped):
    summed = jnp.zeros(padded.shape[:1] + (row_count, col_count, padded.shape[3]), jnp.float32)
    for row_off in range(3):
        for col_off in range(3):
            if flipped:
                window = padded[
                    :, 2 - row_off : 2 - row_off + row_count, 2 - col_off : 2 - col_off + col_count
                ]
            else:
                window = padded[:, row_off : row_off + row_count, col_off : col_off + col_count]
            summed = summed + conv_taps[row_off, col_off] * window
    return summed


def add_pair(earlier, later):
    return (earlier[0] + later[0], earlier[1] + later[1])


def shards(query_pre, key_pre, value_pre, grad_out, conv_taps):
    frame_count, row_count, col_count, model_width = value_pre.shape
    head_count = HEADS
    head_size = HEAD_DIM
    token_count = frame_count * row_count * col_count
    split = (token_count, head_count, head_size)
    highest = lax.Precision.HIGHEST
    value_rows, grad_band = (
        extended(value_pre, (("space", 1),), 1),
        extended(grad_out, (("space", 1),), 1),
    )
    value_pad = jnp.pad(value_rows, ((0, 0), (0, 0), (1, 1), (0, 0)))
    local = mix_rows(value_pad, conv_taps, row_count, col_count, False)
    queries = jnp.maximum(query_pre, 0).reshape(split)
    keys = jnp.maximum(key_pre, 0).reshape(split)
    values = value_pre.reshape(split)
    partial_value = jnp.einsum("the,thd->hed", keys, values, preferred_element_type=jnp.float32)
    key_sum = jnp.sum(keys, axis=0, dtype=jnp.float32)
    half_state, half_sum = (
        lax.psum_scatter(partial_value, "space", scatter_dimension=0, tiled=True),
        lax.psum_scatter(key_sum, "space", scatter_dimension=0, tiled=True),
    )
    before = carried_in(
        (half_state, half_sum),
        "tm",
        add_pair,
        (jnp.zeros_like(half_state), jnp.zeros_like(half_sum)),
    )
    kv_state, key_total = (
        lax.all_gather(before[0] + half_state, "space", axis=0, tiled=True),
        lax.all_gather(before[1] + half_sum, "space", axis=0, tiled=True),
    )
    query_f32 = queries.astype(jnp.float32)
    numerator = jnp.einsum("the,hed->thd", query_f32, kv_state, precision=highest)
    denominator = jnp.einsum("the,he->th", query_f32, key_total, precision=highest) + 1.0
    output_f32 = numerator / denominator[..., None]
    attended = (output_f32.reshape(value_pre.shape) + local).astype(jnp.bfloat16)
    cotangent = grad_out.astype(jnp.float32).reshape(split)
    grad_num = cotangent / denominator[..., None]
    grad_den = -jnp.sum(cotangent * output_f32, axis=-1) / denominator
    grad_query = (
        jnp.einsum("thd,hed->the", grad_num, kv_state, precision=highest)
        + grad_den[..., None] * key_total[None]
    )
    grad_partial = jnp.einsum("the,thd->hed", query_f32, grad_num, precision=highest)
    grad_keysum = jnp.einsum("th,the->he", grad_den, query_f32, precision=highest)
    half_grad, half_keysum = (
        lax.psum_scatter(grad_partial, "space", scatter_dimension=0, tiled=True),
        lax.psum_scatter(grad_keysum, "space", scatter_dimension=0, tiled=True),
    )
    after = carried_in_2(
        (half_grad, half_keysum),
        "tm",
        add_pair,
        (jnp.zeros_like(half_grad), jnp.zeros_like(half_keysum)),
    )
    grad_state, grad_total = (
        lax.all_gather(
            (after[0] + half_grad).astype(jnp.bfloat16), "space", axis=0, tiled=True
        ).astype(jnp.float32),
        lax.all_gather(
            (after[1] + half_keysum).astype(jnp.bfloat16), "space", axis=0, tiled=True
        ).astype(jnp.float32),
    )
    grad_key = (
        jnp.einsum("thd,hed->the", values.astype(jnp.float32), grad_state, precision=highest)
        + grad_total[None]
    )
    grad_mixed = jnp.einsum(
        "the,hed->thd", keys.astype(jnp.float32), grad_state, precision=highest
    ).reshape(value_pre.shape)
    query_grad = jnp.where(query_pre > 0, grad_query.reshape(value_pre.shape), 0.0).astype(
        jnp.bfloat16
    )
    key_grad = jnp.where(key_pre > 0, grad_key.reshape(value_pre.shape), 0.0).astype(jnp.bfloat16)
    grad_pad = jnp.pad(grad_band, ((0, 0), (0, 0), (1, 1), (0, 0)))
    value_grad = (grad_mixed + mix_rows(grad_pad, conv_taps, row_count, col_count, True)).astype(
        jnp.bfloat16
    )
    cotangent_full = grad_out.astype(jnp.float32)
    tap_rows = []
    for row_off in range(3):
        tap_cols = []
        for col_off in range(3):
            window = value_pad[:, row_off : row_off + row_count, col_off : col_off + col_count]
            tap_cols.append(jnp.sum(cotangent_full * window, axis=(0, 1, 2)))
        tap_rows.append(jnp.stack(tap_cols))
    taps_grad = lax.psum(jnp.stack(tap_rows), ("tm", "space"))
    return (attended, query_grad, key_grad, value_grad, taps_grad)


def solution(mesh):
    return jax.shard_map(
        shards,
        mesh=mesh,
        in_specs=(
            P(("groups", "tm"), "space", None, None),
            P(("groups", "tm"), "space", None, None),
            P(("groups", "tm"), "space", None, None),
            P(("groups", "tm"), "space", None, None),
            P(),
        ),
        out_specs=(
            P(("groups", "tm"), "space", None, None),
            P(("groups", "tm"), "space", None, None),
            P(("groups", "tm"), "space", None, None),
            P(("groups", "tm"), "space", None, None),
            P("groups", None, None),
        ),
        check_vma=False,
    )
```

profile of v0, /device:TPU:8, one launch (start us, length us, event | category | flops | bytes accessed | tf_op | source)
XLA Modules:
  0.0 254.5 jit_solution(9472925568814212947)
XLA Ops:
  13.3 10.1 %reduce-scatter.7.cloned.1.call-done = f32[10,112,112]{2,1,0:T(8,128)} async-done(((f32[20,112,112]{2,1,0:T(8,128)}), f32[10,112,112]{2,1,0:T(8,128)}) %reduce-scatter.7.cloned.1.call-update) | async-done | bytes 501776 | tf_op jit(solution)/shard_map/reduce_scatter | solution.py:96
  23.7 2.7 %fusion = f32[16,112]{1,0:T(8,128)S(1)} fusion(f32[20,112]{1,0:T(8,128)S(1)} %reduce_sum.102), kind=kCustom, calls=%all-reduce-scatter | all-reduce-scatter fusion | flops 3585 | bytes 16640
  26.4 2.2 collective-permute-start.4
  33.0 2.0 reshape.72
  35.7 28.8 %all-gather.4 = f32[8,10,112]{2,1,0:T(8,128)S(1)} all-gather(f32[1,10,112]{2,1,0:T(8,128)S(1)} %fusion.37), channel_id=3, replica_groups=mesh['groups'=2,'tm'=8,'space'=2] {'tm'}, dimensions={0}, use_global_device_ids=true | all-gather | bytes 40320 | tf_op jit(solution)/shard_map/all_gather | solution.py:25
  64.5 39.8 %all-gather.11.cloned.1.call-done = f32[80,112,112]{2,1,0:T(8,128)} async-done(((f32[10,112,112]{2,1,0:T(8,128)}), f32[80,112,112]{2,1,0:T(8,128)}) %all-gather.11.cloned.1.call-update) | async-done | bytes 4014096 | tf_op jit(solution)/shard_map/all_gather | solution.py:25
  104.3 2.5 while.26
  110.0 2.4 fusion.33
  112.5 13.9 %reduce-scatter.9.cloned.1.call-done = f32[10,112,112]{2,1,0:T(8,128)} async-done(((f32[20,112,112]{2,1,0:T(8,128)}), f32[10,112,112]{2,1,0:T(8,128)}) %reduce-scatter.9.cloned.1.call-update) | async-done | bytes 501776 | tf_op jit(solution)/shard_map/reduce_scatter | solution.py:124
  129.6 3.0 %collective-permute-start = (bf16[1,1,32,2240]{3,2,1,0:T(8,128)(2,1)S(1)}, bf16[1,1,32,2240]{3,2,1,0:T(8,128)(2,1)S(1)}, u32[]{:S(2)}, u32[]{:S(2)}) collective-permute-start(bf16[1,1,32,2240]{3,2,1,0:T(8,128)(2,1)S(1)} %get-tuple-element.171), channel_id=1, source_target_pairs={{0,1},{2,3},{4,5},{6,7},{8,9},{10,11},{12,13},{14,15},{16,17},{18,... | collective-permute-start | bytes 430088 | tf_op jit(solution)/shard_map/ppermute | solution.py:15
  134.7 3.7 %collective-permute-start.2 = (bf16[1,1,32,2240]{3,2,1,0:T(8,128)(2,1)}, bf16[1,1,32,2240]{3,2,1,0:T(8,128)(2,1)}, u32[]{:S(2)}, u32[]{:S(2)}) collective-permute-start(bf16[1,1,32,2240]{3,2,1,0:T(8,128)(2,1)} %get-tuple-element.169), channel_id=1, source_target_pairs={{0,1},{2,3},{4,5},{6,7},{8,9},{10,11},{12,13},{14,15},{16,17},{18,... | collective-permute-start | bytes 430088 | tf_op jit(solution)/shard_map/ppermute | solution.py:15
  145.5 2.9 %all_gather.40 = f32[20,112,112]{2,1,0:T(8,128)S(1)} all-gather(f32[10,112,112]{2,1,0:T(8,128)S(1)} %add.145), channel_id=1, replica_groups=mesh['groups'=2,'tm'=8,'space'=2] {'space'}, dimensions={0}, use_global_device_ids=true | all-gather | bytes 1505280 | tf_op jit(solution)/shard_map/all_gather | solution.py:106
  148.5 2.7 %multiply_reduce_fusion = (f32[128,20]{0,1:T(8,128)}, f32[128,20,112]{0,2,1:T(8,128)}) fusion(f32[128,20,112]{0,2,1:T(8,128)S(1)} %copy-done.18, f32[128,20]{0,1:T(8,128)S(1)} %copy-done.37, f32[20,112,112]{2,1,0:T(8,128)S(1)} %all_gather.40, bf16[128,20,112]{0,2,1:T(8,128)(2,1)S(1)} %copy-done.10), kind=kOutput, calls=%fused_computation.62 | convolution fusion | flops 386209280 | bytes 3891200 | tf_op jit(solution)/shard_map/the,hed->thd/dot_general | solution.py:110
  151.2 2.9 %copy.41 = f32[128,20,112]{2,1,0:T(8,128)} copy(f32[128,20,112]{0,2,1:T(8,128)} %get-tuple-element.174) | data formatting | bytes 2293760 | tf_op jit(solution)/shard_map/div | solution.py:112
  154.2 2.7 %reshape.73 = f32[1,4,32,2240]{3,2,1,0:T(8,128)} reshape(f32[128,20,112]{2,1,0:T(8,128)} %copy.41) | data formatting | bytes 2293760 | tf_op jit(solution)/shard_map/reshape | solution.py:113
  158.6 2.7 %fusion.1 = f32[16,112]{1,0:T(8,128)S(1)} fusion(f32[20,112]{1,0:T(8,128)S(1)} %bitcast.88), kind=kCustom, calls=%all-reduce-scatter.1 | all-reduce-scatter fusion | flops 3585 | bytes 16640
  161.3 2.2 collective-permute-start.5
  163.6 3.3 %fusion.15 = bf16[1,4,32,2240]{3,2,1,0:T(8,128)(2,1)} fusion(f32[1,4,32,2240]{3,2,1,0:T(8,128)} %reshape.73, bf16[1,4,32,2240]{3,2,1,0:T(8,128)(2,1)S(1)} %copy-done, bf16[1,1,32,2240]{3,2,1,0:T(8,128)(2,1)S(1)} %collective-permute-done.1, bf16[1,1,32,2240]{3,2,1,0:T(8,128)(2,1)} %copy-done.14, f32[2240]{0:T(1024)} %get-tuple-element.143, ...), kind=kLoop, calls=%fused_computation.42 | loop fusion | flops 8601600 | bytes 6101760 | tf_op jit(solution)/shard_map/convert_element_type | solution.py:113
  170.3 28.0 %all-gather.6 = bf16[8,10,112]{2,1,0:T(8,128)(2,1)S(1)} all-gather(bf16[1,10,112]{2,1,0:T(8,128)(2,1)S(1)} %fusion.39), channel_id=5, replica_groups=mesh['groups'=2,'tm'=8,'space'=2] {'tm'}, dimensions={0}, use_global_device_ids=true | all-gather | bytes 20160 | tf_op jit(solution)/shard_map/all_gather | solution.py:41
  198.4 5.6 %while.27 = (s32[]{:T(128)}, f32[10,112,112]{2,1,0:T(8,128)S(1)}, f32[10,112]{1,0:T(8,128)S(1)}, s32[]{:T(128)}, bf16[8,10,112,112]{3,2,1,0:T(8,128)(2,1)}, /*in...) while((s32[]{:T(128)}, f32[10,112,112]{2,1,0:T(8,128)S(1)}, ...), condition=%wide.region_9.10_spmd, body=%wide.region_8.9_spmd.sunk | while | flops 253126 | bytes 1265763 | solution.py:56
  204.1 2.3 all_gather.46
  217.7 2.8 %select_convert_fusion = (bf16[1,4,32,2240]{3,2,1,0:T(8,128)(2,1)}, bf16[1,4,32,2240]{3,2,1,0:T(8,128)(2,1)}) fusion(bf16[1,4,32,2240]{3,2,1,0:T(8,128)(2,1)} %reshape.76, bf16[1,4,32,2240]{3,2,1,0:T(8,128)(2,1)S(1)} %copy-done.4, bf16[1,4,32,2240]{3,2,1,0:T(8,128)(2,1)} %reshape.75, bf16[1,4,32,2240]{3,2,1,0:T(8,128)(2,1)} %param.9), kind=kLoop, calls=%fused_computation.59 | loop fusion | flops 2007040 | bytes 3440640 | tf_op jit(solution)/shard_map/convert_element_type | solution.py:151
  220.6 2.7 %fusion.22 = bf16[1,4,32,2240]{3,2,1,0:T(8,128)(2,1)} fusion(f32[1,4,32,2240]{3,2,1,0:T(8,128)S(1)} %reshape.77, bf16[1,4,32,2240]{3,2,1,0:T(8,128)(2,1)S(1)} %copy-done.2, bf16[1,6,34,2240]{3,2,1,0:T(8,128)(2,1)S(1)} %select_maximum_fusion, bf16[1,1,32,2240]{3,2,1,0:T(8,128)(2,1)} %collective-permute-done.2, bf16[1,1,32,2240]{3,2,1,0:T(8,128)(2,1)S(1)} %copy-done.21, ...), kind=kLoop, calls=%fused_computation.49 | loop fusion | flops 8601600 | bytes 6101760 | tf_op jit(solution)/shard_map/convert_element_type | solution.py:153
  223.3 22.5 %all-reduce.8.cloned.1.call-done = f32[3,3,2240]{2,1,0:T(4,128)} async-done(((f32[3,3,2240]{2,1,0:T(4,128)}), f32[3,3,2240]{2,1,0:T(4,128)}) %all-reduce.8.cloned.1.call-update) | async-done | bytes 80656 | tf_op jit(solution)/shard_map/psum | solution.py:164
  (179 shorter events, 51.2 us)
Async XLA Ops:
  8.0 15.4 %reduce-scatter.7.cloned.1.call-start = ((), (), s32[]{:S(2)}) async-start(), calls=%async_computation.2 | async-start | bytes 1720320 | tf_op jit(solution)/shard_map/reduce_scatter | solution.py:96
  13.3 10.3 %copy-start.3 = (bf16[1,4,32,2240]{3,2,1,0:T(8,128)(2,1)S(1)}, bf16[1,4,32,2240]{3,2,1,0:T(8,128)(2,1)}, u32[]{:S(2)}) copy-start(bf16[1,4,32,2240]{3,2,1,0:T(8,128)(2,1)} %param.10) | copy-start | bytes 1720324
  13.3 15.4 %copy-start.12 = (bf16[1,4,32,2240]{3,2,1,0:T(8,128)(2,1)S(1)}, bf16[1,4,32,2240]{3,2,1,0:T(8,128)(2,1)}, u32[]{:S(2)}) copy-start(bf16[1,4,32,2240]{3,2,1,0:T(8,128)(2,1)} %param.9) | copy-start | bytes 1720324
  13.3 91.0 %all-gather.11.cloned.1.call-start = ((), (), s32[]{:S(2)}) async-start(), calls=%async_computation.5 | async-start | bytes 5160960 | tf_op jit(solution)/shard_map/all_gather | solution.py:25
  23.4 6.1 %copy-start.1 = (bf16[1,4,32,2240]{3,2,1,0:T(8,128)(2,1)S(1)}, bf16[1,4,32,2240]{3,2,1,0:T(8,128)(2,1)}, u32[]{:S(2)}) copy-start(bf16[1,4,32,2240]{3,2,1,0:T(8,128)(2,1)} %param.12) | copy-start | bytes 1720324
  23.5 102.9 %reduce-scatter.9.cloned.1.call-start = ((), (), s32[]{:S(2)}) async-start(), calls=%async_computation.3 | async-start | bytes 1720320 | tf_op jit(solution)/shard_map/reduce_scatter | solution.py:124
  26.4 9.1 %collective-permute-start.4 = (f32[6,112]{1,0:T(8,128)S(1)}, f32[6,112]{1,0:T(8,128)S(1)}, u32[]{:S(2)}, u32[]{:S(2)}) collective-permute-start(f32[6,112]{1,0:T(8,128)S(1)} %slice.158), channel_id=1, source_target_pairs={{0,1},{2,3},{4,5},{6,7},{8,9},{10,11},{12,13},{14,15},{16,17},{18,... | collective-permute-start | bytes 8072
  35.5 74.5 %copy-start.9 = (bf16[128,20,112]{0,2,1:T(8,128)(2,1)}, bf16[128,20,112]{0,2,1:T(8,128)(2,1)S(1)}, u32[]{:S(2)}) copy-start(bf16[128,20,112]{0,2,1:T(8,128)(2,1)S(1)} %copy.40) | copy-start | bytes 1720324
  35.7 68.6 %copy-start.31 = (f32[22,112]{1,0:T(8,128)}, f32[22,112]{1,0:T(8,128)S(1)}, u32[]{:S(2)}) copy-start(f32[22,112]{1,0:T(8,128)S(1)} %concatenate.24) | copy-start | bytes 29572
  104.3 5.7 %copy-start.17 = (f32[128,20,112]{0,2,1:T(8,128)S(1)}, f32[128,20,112]{0,2,1:T(8,128)}, u32[]{:S(2)}) copy-start(f32[128,20,112]{0,2,1:T(8,128)} %copy.42) | copy-start | bytes 3440644
  112.4 26.0 %copy-start.32 = (f32[3,3,2240]{2,1,0:T(4,128)S(1)}, f32[3,3,2240]{2,1,0:T(4,128)}, u32[]{:S(2)}) copy-start(f32[3,3,2240]{2,1,0:T(4,128)} %param.13) | copy-start | bytes 241924
  112.4 85.9 %all-gather.13.cloned.1.call-start = ((), (), s32[]{:S(2)}) async-start(), calls=%async_computation.6 | async-start | bytes 2580480 | tf_op jit(solution)/shard_map/all_gather | solution.py:41
  128.2 117.6 %all-reduce.8.cloned.1.call-start = ((), (), s32[]{:S(2)}) async-start(), calls=%async_computation.4 | async-start | bytes 221184 | tf_op jit(solution)/shard_map/psum | solution.py:164
  128.3 10.9 %collective-permute-start.1 = (bf16[1,1,32,2240]{3,2,1,0:T(8,128)(2,1)S(1)}, bf16[1,1,32,2240]{3,2,1,0:T(8,128)(2,1)S(1)}, u32[]{:S(2)}, u32[]{:S(2)}) collective-permute-start(bf16[1,1,32,2240]{3,2,1,0:T(8,128)(2,1)S(1)} %get-tuple-element.172), channel_id=1, source_target_pairs={{1,0},{3,2},{5,4},{7,6},{9,8},{11,10},{13,12},{15,14},{17,16},{19,... | collective-permute-start | bytes 430088 | tf_op jit(solution)/shard_map/ppermute | solution.py:18
  129.6 9.6 %collective-permute-start = (bf16[1,1,32,2240]{3,2,1,0:T(8,128)(2,1)S(1)}, bf16[1,1,32,2240]{3,2,1,0:T(8,128)(2,1)S(1)}, u32[]{:S(2)}, u32[]{:S(2)}) collective-permute-start(bf16[1,1,32,2240]{3,2,1,0:T(8,128)(2,1)S(1)} %get-tuple-element.171), channel_id=1, source_target_pairs={{0,1},{2,3},{4,5},{6,7},{8,9},{10,11},{12,13},{14,15},{16,17},{18,... | collective-permute-start | bytes 430088 | tf_op jit(solution)/shard_map/ppermute | solution.py:15
  133.4 8.2 %collective-permute-start.3 = (bf16[1,1,32,2240]{3,2,1,0:T(8,128)(2,1)}, bf16[1,1,32,2240]{3,2,1,0:T(8,128)(2,1)S(1)}, u32[]{:S(2)}, u32[]{:S(2)}) collective-permute-start(bf16[1,1,32,2240]{3,2,1,0:T(8,128)(2,1)} %get-tuple-element.170), channel_id=1, source_target_pairs={{1,0},{3,2},{5,4},{7,6},{9,8},{11,10},{13,12},{15,14},{17,16},{19,... | collective-permute-start | bytes 430088 | tf_op jit(solution)/shard_map/ppermute | solution.py:18
  134.7 7.6 %collective-permute-start.2 = (bf16[1,1,32,2240]{3,2,1,0:T(8,128)(2,1)}, bf16[1,1,32,2240]{3,2,1,0:T(8,128)(2,1)}, u32[]{:S(2)}, u32[]{:S(2)}) collective-permute-start(bf16[1,1,32,2240]{3,2,1,0:T(8,128)(2,1)} %get-tuple-element.169), channel_id=1, source_target_pairs={{0,1},{2,3},{4,5},{6,7},{8,9},{10,11},{12,13},{14,15},{16,17},{18,... | collective-permute-start | bytes 430088 | tf_op jit(solution)/shard_map/ppermute | solution.py:15
  144.4 4.1 %copy-start.37 = (f32[128,20]{0,1:T(8,128)S(1)}, f32[128,20]{0,1:T(8,128)}, u32[]{:S(2)}) copy-start(f32[128,20]{0,1:T(8,128)} %copy-done.36) | copy-start | bytes 30724
  154.1 9.4 %copy-start.22 = (f32[2240]{0:T(1024)S(1)}, f32[2240]{0:T(1024)}, u32[]{:S(2)}) copy-start(f32[2240]{0:T(1024)} %get-tuple-element.137) | copy-start | bytes 26884
  161.3 8.9 %collective-permute-start.5 = (f32[6,112]{1,0:T(8,128)S(1)}, f32[6,112]{1,0:T(8,128)S(1)}, u32[]{:S(2)}, u32[]{:S(2)}) collective-permute-start(f32[6,112]{1,0:T(8,128)S(1)} %slice.159), channel_id=1, source_target_pairs={{0,1},{2,3},{4,5},{6,7},{8,9},{10,11},{12,13},{14,15},{16,17},{18,... | collective-permute-start | bytes 8072
  163.5 3.4 %copy-start.16 = (f32[20,112,112]{2,1,0:T(8,128)S(1)}, f32[20,112,112]{2,1,0:T(8,128)}, u32[]{:S(2)}) copy-start(f32[20,112,112]{2,1,0:T(8,128)} %copy-done.15) | copy-start | bytes 3010564
  163.5 3.4 %copy-start.19 = (f32[128,20,112]{0,2,1:T(8,128)S(1)}, f32[128,20,112]{0,2,1:T(8,128)}, u32[]{:S(2)}) copy-start(f32[128,20,112]{0,2,1:T(8,128)} %copy.42) | copy-start | bytes 3440644
  198.4 5.6 %copy-start.13 = (f32[10,112,112]{2,1,0:T(8,128)S(1)}, f32[10,112,112]{2,1,0:T(8,128)}, u32[]{:S(2)}) copy-start(f32[10,112,112]{2,1,0:T(8,128)} %reduce-scatter.9.cloned.1.call-done) | copy-start | bytes 1505284
  204.0 4.4 %copy-start.6 = (bf16[128,20,112]{0,2,1:T(8,128)(2,1)S(1)}, bf16[128,20,112]{0,2,1:T(8,128)(2,1)}, u32[]{:S(2)}) copy-start(bf16[128,20,112]{0,2,1:T(8,128)(2,1)} %copy-done.5) | copy-start | bytes 1720324
  (27 other events, 66.7 us)
Sparse Core Ops, SparseCore 0:
  13.4 9.9 reduce-scatter.6
  25.6 78.6 all-gather.10
  112.5 13.7 reduce-scatter.8
  128.4 52.3 all-gather.12
Sparse Core Ops, SparseCore 1:
  141.7 104.1 all-reduce.7
where the time goes:
time: 256 us; the launch traced here: 255 us
  waiting for transfers between devices  86.4 us (34%)
  blocking collectives  71.2 us (28%)
  other arithmetic  27.1 us (11%)
  local copies, waits for them, and re-layouts  26.9 us (11%)
  between operations  16.6 us (6%)
  starting transfers between devices  14 us (5%)
  matrix products  12.1 us (5%)
    all_gather x1, waiting for transfers between devices, carried_in(): gathered = jax.tree.map(lambda a: lax.all_gather(a, axis), part)  39.8 us
    all_gather x1, blocking collectives, carried_in(): gathered = jax.tree.map(lambda a: lax.all_gather(a, axis), part)  28.8 us
    all_gather x1, blocking collectives, carried_in_2(): lax.all_gather(a.astype(kind), axis)  28 us
    psum x1, waiting for transfers between devices, shards(): taps_grad = lax.psum(jnp.stack(tap_rows), ('tm', 'space'))  22.5 us
    reduce_scatter x1, waiting for transfers between devices, shards(): lax.psum_scatter(grad_partial, 'space', scatter_dimension=0, tiled=True)  13.9 us
    reduce_scatter x1, waiting for transfers between devices, shards(): lax.psum_scatter(partial_value, 'space', scatter_dimension=0, tiled=True)  10.1 us
    add x14, other arithmetic, add_pair(): return (earlier[0] + later[0], earlier[1] + later[1])  7.9 us
    ppermute x2, starting transfers between devices, extended(): lax.ppermute(lax.slice_in_dim(block, block.shape[dim] - width, None, axis...  6.74 us
  transfers between devices with their start and end apart: 11, of which 4 were waited for; matrix products, arithmetic and copies ran while one was open for 22% of the time, Pallas kernels for 0%

commit v1 on v0

--- a/solution.py
+++ b/solution.py
@@ -161,7 +161,7 @@
             window = value_pad[:, row_off : row_off + row_count, col_off : col_off + col_count]
             tap_cols.append(jnp.sum(cotangent_full * window, axis=(0, 1, 2)))
         tap_rows.append(jnp.stack(tap_cols))
-    taps_grad = lax.psum(jnp.stack(tap_rows), ("tm", "space"))
+    taps_grad = jnp.sum(lax.all_gather(jnp.stack(tap_rows), ("tm", "space")), axis=0)
     return (attended, query_grad, key_grad, value_grad, taps_grad)
 
 

time: 256 us -> 264 us (1.031)
  the two profiles are of different devices: /device:TPU:8 before, /device:TPU:0 now
where the time goes in v1:
time: 264 us; the launch traced here: 262 us
  waiting for transfers between devices  87.2 us (33%)
  blocking collectives  77.7 us (29%)
  other arithmetic  27.7 us (10%)
  local copies, waits for them, and re-layouts  25.9 us (10%)
  between operations  16.6 us (6%)
  starting transfers between devices  13.8 us (5%)
  matrix products  13.4 us (5%)
    all_gather x1, waiting for transfers between devices, carried_in(): gathered = jax.tree.map(lambda a: lax.all_gather(a, axis), part)  37.5 us
    all_gather x1, blocking collectives, carried_in(): gathered = jax.tree.map(lambda a: lax.all_gather(a, axis), part)  31.9 us
    all_gather x1, blocking collectives, carried_in_2(): lax.all_gather(a.astype(kind), axis)  31.1 us
    all_gather x1, waiting for transfers between devices, shards(): lax.all_gather(jnp.stack(tap_rows), ('tm', 'space'))  29.7 us
    reduce_scatter x1, waiting for transfers between devices, shards(): lax.psum_scatter(partial_value, 'space', scatter_dimension=0, tiled=True)  11.3 us
    reduce_scatter x1, waiting for transfers between devices, shards(): lax.psum_scatter(grad_partial, 'space', scatter_dimension=0, tiled=True)  7.66 us
    add x14, other arithmetic, add_pair(): return (earlier[0] + later[0], earlier[1] + later[1])  7.58 us
    ppermute x2, starting transfers between devices, extended(): lax.ppermute(lax.slice_in_dim(block, block.shape[dim] - width, None, axis...  6.74 us
  transfers between devices with their start and end apart: 11, of which 5 were waited for; matrix products, arithmetic and copies ran while one was open for 15% of the time, Pallas kernels for 0%

profile of v1, /device:TPU:0, one launch (start us, length us, event | category | flops | bytes accessed | tf_op | source)
XLA Modules:
  0.0 262.4 jit_solution(17662649459920691666)
XLA Ops:
  14.1 11.3 %reduce-scatter.7.cloned.1.call-done = f32[10,112,112]{2,1,0:T(8,128)} async-done(((f32[20,112,112]{2,1,0:T(8,128)}), f32[10,112,112]{2,1,0:T(8,128)}) %reduce-scatter.7.cloned.1.call-update) | async-done | bytes 501776 | tf_op jit(solution)/shard_map/reduce_scatter | solution.py:96
  25.7 2.8 %fusion = f32[16,112]{1,0:T(8,128)S(1)} fusion(f32[20,112]{1,0:T(8,128)S(1)} %reduce_sum.111), kind=kCustom, calls=%all-reduce-scatter | all-reduce-scatter fusion | flops 3585 | bytes 16640
  28.6 2.1 collective-permute-start.4
  37.7 31.9 %all-gather.5 = f32[8,10,112]{2,1,0:T(8,128)S(1)} all-gather(f32[1,10,112]{2,1,0:T(8,128)S(1)} %fusion.37), channel_id=3, replica_groups=mesh['groups'=2,'tm'=8,'space'=2] {'tm'}, dimensions={0}, use_global_device_ids=true | all-gather | bytes 40320 | tf_op jit(solution)/shard_map/all_gather | solution.py:25
  69.6 37.5 %all-gather.13.cloned.1.call-done = f32[80,112,112]{2,1,0:T(8,128)} async-done(((f32[10,112,112]{2,1,0:T(8,128)}), f32[80,112,112]{2,1,0:T(8,128)}) %all-gather.13.cloned.1.call-update) | async-done | bytes 4014096 | tf_op jit(solution)/shard_map/all_gather | solution.py:25
  109.6 3.6 %fusion.33 = f32[20,112,112]{2,1,0:T(8,128)} fusion(bf16[128,20,112]{0,2,1:T(8,128)(2,1)S(1)} %copy.40, f32[128,20,112]{0,2,1:T(8,128)} %copy.42, f32[128,20]{0,1:T(8,128)S(1)} %fusion.34), kind=kOutput, calls=%fused_computation.74 | convolution fusion | flops 385638400 | bytes 2734080 | tf_op jit(solution)/shard_map/the,thd->hed/dot_general | solution.py:121
  114.6 3.0 %collective-permute-start = (bf16[1,1,32,2240]{3,2,1,0:T(8,128)(2,1)S(1)}, bf16[1,1,32,2240]{3,2,1,0:T(8,128)(2,1)S(1)}, u32[]{:S(2)}, u32[]{:S(2)}) collective-permute-start(bf16[1,1,32,2240]{3,2,1,0:T(8,128)(2,1)S(1)} %get-tuple-element.171), channel_id=1, source_target_pairs={{0,1},{2,3},{4,5},{6,7},{8,9},{10,11},{12,13},{14,15},{16,17},{18,... | collective-permute-start | bytes 430088 | tf_op jit(solution)/shard_map/ppermute | solution.py:15
  121.1 7.7 %reduce-scatter.9.cloned.1.call-done = f32[10,112,112]{2,1,0:T(8,128)} async-done(((f32[20,112,112]{2,1,0:T(8,128)}), f32[10,112,112]{2,1,0:T(8,128)}) %reduce-scatter.9.cloned.1.call-update) | async-done | bytes 501776 | tf_op jit(solution)/shard_map/reduce_scatter | solution.py:124
  132.0 3.7 %collective-permute-start.2 = (bf16[1,1,32,2240]{3,2,1,0:T(8,128)(2,1)S(1)}, bf16[1,1,32,2240]{3,2,1,0:T(8,128)(2,1)}, u32[]{:S(2)}, u32[]{:S(2)}) collective-permute-start(bf16[1,1,32,2240]{3,2,1,0:T(8,128)(2,1)S(1)} %get-tuple-element.169), channel_id=1, source_target_pairs={{0,1},{2,3},{4,5},{6,7},{8,9},{10,11},{12,13},{14,15},{16,17},{18,... | collective-permute-start | bytes 430088 | tf_op jit(solution)/shard_map/ppermute | solution.py:15
  138.7 29.7 %all-gather.17.cloned.1.call-done = f32[48,3,2240]{2,1,0:T(4,128)} async-done(((f32[3,3,2240]{2,1,0:T(4,128)}), f32[48,3,2240]{2,1,0:T(4,128)}) %all-gather.17.cloned.1.call-update) | async-done | bytes 1290256 | tf_op jit(solution)/shard_map/all_gather | solution.py:164
  168.4 2.4 reduce_sum.122
  172.6 2.9 %all_gather.46 = f32[20,112,112]{2,1,0:T(8,128)S(1)} all-gather(f32[10,112,112]{2,1,0:T(8,128)S(1)} %add.143), channel_id=1, replica_groups=mesh['groups'=2,'tm'=8,'space'=2] {'space'}, dimensions={0}, use_global_device_ids=true | all-gather | bytes 1505280 | tf_op jit(solution)/shard_map/all_gather | solution.py:106
  175.5 2.7 %multiply_reduce_fusion = (f32[128,20]{0,1:T(8,128)}, f32[128,20,112]{0,2,1:T(8,128)}) fusion(f32[128,20,112]{0,2,1:T(8,128)S(1)} %copy-done.17, f32[128,20]{0,1:T(8,128)S(1)} %copy-done.37, f32[20,112,112]{2,1,0:T(8,128)S(1)} %all_gather.46, bf16[128,20,112]{0,2,1:T(8,128)(2,1)S(1)} %copy-done.10), kind=kOutput, calls=%fused_computation.62 | convolution fusion | flops 386209280 | bytes 3891200 | tf_op jit(solution)/shard_map/the,hed->thd/dot_general | solution.py:110
  178.2 2.9 %copy.41 = f32[128,20,112]{2,1,0:T(8,128)} copy(f32[128,20,112]{0,2,1:T(8,128)} %get-tuple-element.174) | data formatting | bytes 2293760 | tf_op jit(solution)/shard_map/div | solution.py:112
  181.2 2.7 %reshape.73 = f32[1,4,32,2240]{3,2,1,0:T(8,128)} reshape(f32[128,20,112]{2,1,0:T(8,128)} %copy.41) | data formatting | bytes 2293760 | tf_op jit(solution)/shard_map/reshape | solution.py:113
  185.6 2.7 %fusion.1 = f32[16,112]{1,0:T(8,128)S(1)} fusion(f32[20,112]{1,0:T(8,128)S(1)} %bitcast.90), kind=kCustom, calls=%all-reduce-scatter.1 | all-reduce-scatter fusion | flops 3585 | bytes 16640
  188.3 2.2 collective-permute-start.5
  190.6 3.3 %fusion.15 = bf16[1,4,32,2240]{3,2,1,0:T(8,128)(2,1)} fusion(f32[1,4,32,2240]{3,2,1,0:T(8,128)} %reshape.73, bf16[1,4,32,2240]{3,2,1,0:T(8,128)(2,1)S(1)} %copy-done, bf16[1,1,32,2240]{3,2,1,0:T(8,128)(2,1)S(1)} %collective-permute-done.1, bf16[1,1,32,2240]{3,2,1,0:T(8,128)(2,1)} %copy-done.14, f32[2240]{0:T(1024)} %get-tuple-element.143, ...), kind=kLoop, calls=%fused_computation.42 | loop fusion | flops 8601600 | bytes 6101760 | tf_op jit(solution)/shard_map/convert_element_type | solution.py:113
  197.4 31.1 %all-gather.7 = bf16[8,10,112]{2,1,0:T(8,128)(2,1)S(1)} all-gather(bf16[1,10,112]{2,1,0:T(8,128)(2,1)S(1)} %fusion.39), channel_id=5, replica_groups=mesh['groups'=2,'tm'=8,'space'=2] {'tm'}, dimensions={0}, use_global_device_ids=true | all-gather | bytes 20160 | tf_op jit(solution)/shard_map/all_gather | solution.py:41
  228.6 7.8 %while.27 = (s32[]{:T(128)}, f32[10,112,112]{2,1,0:T(8,128)S(1)}, f32[10,112]{1,0:T(8,128)S(1)}, s32[]{:T(128)}, bf16[8,10,112,112]{3,2,1,0:T(8,128)(2,1)}, /*in...) while((s32[]{:T(128)}, f32[10,112,112]{2,1,0:T(8,128)S(1)}, ...), condition=%wide.region_9.10_spmd, body=%wide.region_8.9_spmd.sunk | while | flops 253126 | bytes 1265763 | solution.py:56
  236.4 2.3 all_gather.52
  238.8 1.9 all-gather.8
  249.6 2.9 %select_convert_fusion = (bf16[1,4,32,2240]{3,2,1,0:T(8,128)(2,1)}, bf16[1,4,32,2240]{3,2,1,0:T(8,128)(2,1)}) fusion(bf16[1,4,32,2240]{3,2,1,0:T(8,128)(2,1)} %reshape.76, bf16[1,4,32,2240]{3,2,1,0:T(8,128)(2,1)S(1)} %copy-done.4, bf16[1,4,32,2240]{3,2,1,0:T(8,128)(2,1)} %reshape.75, bf16[1,4,32,2240]{3,2,1,0:T(8,128)(2,1)} %param.9), kind=kLoop, calls=%fused_computation.59 | loop fusion | flops 2007040 | bytes 3440640 | tf_op jit(solution)/shard_map/convert_element_type | solution.py:151
  252.6 2.7 %fusion.22 = bf16[1,4,32,2240]{3,2,1,0:T(8,128)(2,1)} fusion(f32[1,4,32,2240]{3,2,1,0:T(8,128)S(1)} %copy-done.11, bf16[1,4,32,2240]{3,2,1,0:T(8,128)(2,1)S(1)} %copy-done.2, bf16[1,6,34,2240]{3,2,1,0:T(8,128)(2,1)S(1)} %select_maximum_fusion, bf16[1,1,32,2240]{3,2,1,0:T(8,128)(2,1)} %collective-permute-done.2, bf16[1,1,32,2240]{3,2,1,0:T(8,128)(2,1)S(1)} %copy-done.20, ...), kind=kLoop, calls=%fused_computation.49 | loop fusion | flops 8601600 | bytes 6101760 | tf_op jit(solution)/shard_map/convert_element_type | solution.py:153
  (179 shorter events, 49.4 us)
Async XLA Ops:
  8.0 17.4 %reduce-scatter.7.cloned.1.call-start = ((), (), s32[]{:S(2)}) async-start(), calls=%async_computation.2 | async-start | bytes 1720320 | tf_op jit(solution)/shard_map/reduce_scatter | solution.py:96
  14.1 11.4 %copy-start.3 = (bf16[1,4,32,2240]{3,2,1,0:T(8,128)(2,1)S(1)}, bf16[1,4,32,2240]{3,2,1,0:T(8,128)(2,1)}, u32[]{:S(2)}) copy-start(bf16[1,4,32,2240]{3,2,1,0:T(8,128)(2,1)} %param.10) | copy-start | bytes 1720324
  14.1 16.6 %copy-start.12 = (bf16[1,4,32,2240]{3,2,1,0:T(8,128)(2,1)S(1)}, bf16[1,4,32,2240]{3,2,1,0:T(8,128)(2,1)}, u32[]{:S(2)}) copy-start(bf16[1,4,32,2240]{3,2,1,0:T(8,128)(2,1)} %param.9) | copy-start | bytes 1720324
  14.1 93.0 %all-gather.13.cloned.1.call-start = ((), (), s32[]{:S(2)}) async-start(), calls=%async_computation.4 | async-start | bytes 5160960 | tf_op jit(solution)/shard_map/all_gather | solution.py:25
  25.4 5.3 %copy-start.1 = (bf16[1,4,32,2240]{3,2,1,0:T(8,128)(2,1)S(1)}, bf16[1,4,32,2240]{3,2,1,0:T(8,128)(2,1)}, u32[]{:S(2)}) copy-start(bf16[1,4,32,2240]{3,2,1,0:T(8,128)(2,1)} %param.12) | copy-start | bytes 1720324
  25.4 103.4 %reduce-scatter.9.cloned.1.call-start = ((), (), s32[]{:S(2)}) async-start(), calls=%async_computation.3 | async-start | bytes 1720320 | tf_op jit(solution)/shard_map/reduce_scatter | solution.py:124
  28.6 9.0 %collective-permute-start.4 = (f32[6,112]{1,0:T(8,128)S(1)}, f32[6,112]{1,0:T(8,128)S(1)}, u32[]{:S(2)}, u32[]{:S(2)}) collective-permute-start(f32[6,112]{1,0:T(8,128)S(1)} %slice.158), channel_id=1, source_target_pairs={{0,1},{2,3},{4,5},{6,7},{8,9},{10,11},{12,13},{14,15},{16,17},{18,... | collective-permute-start | bytes 8072
  37.5 72.1 %copy-start.9 = (bf16[128,20,112]{0,2,1:T(8,128)(2,1)}, bf16[128,20,112]{0,2,1:T(8,128)(2,1)S(1)}, u32[]{:S(2)}) copy-start(bf16[128,20,112]{0,2,1:T(8,128)(2,1)S(1)} %copy.40) | copy-start | bytes 1720324
  109.6 3.7 %copy-start.29 = (f32[20,1,128]{2,1,0:T(1,128)}, f32[20,1,128]{2,1,0:T(1,128)S(1)}, u32[]{:S(2)}) copy-start(f32[20,1,128]{2,1,0:T(1,128)S(1)} %fusion.44) | copy-start | bytes 30724
  109.6 3.6 %copy-start.36 = (f32[128,20]{0,1:T(8,128)}, f32[128,20]{0,1:T(8,128)S(1)}, u32[]{:S(2)}) copy-start(f32[128,20]{0,1:T(8,128)S(1)} %fusion.34) | copy-start | bytes 30724
  113.2 55.2 %all-gather.17.cloned.1.call-start = ((), (), s32[]{:S(2)}) async-start(), calls=%async_computation.6 | async-start | bytes 1880064 | tf_op jit(solution)/shard_map/all_gather | solution.py:164
  113.3 4.4 %collective-permute-start.1 = (bf16[1,1,32,2240]{3,2,1,0:T(8,128)(2,1)S(1)}, bf16[1,1,32,2240]{3,2,1,0:T(8,128)(2,1)S(1)}, u32[]{:S(2)}, u32[]{:S(2)}) collective-permute-start(bf16[1,1,32,2240]{3,2,1,0:T(8,128)(2,1)S(1)} %get-tuple-element.172), channel_id=1, source_target_pairs={{1,0},{3,2},{5,4},{7,6},{9,8},{11,10},{13,12},{15,14},{17,16},{19,... | collective-permute-start | bytes 430088 | tf_op jit(solution)/shard_map/ppermute | solution.py:18
  114.6 4.0 %collective-permute-start = (bf16[1,1,32,2240]{3,2,1,0:T(8,128)(2,1)S(1)}, bf16[1,1,32,2240]{3,2,1,0:T(8,128)(2,1)S(1)}, u32[]{:S(2)}, u32[]{:S(2)}) collective-permute-start(bf16[1,1,32,2240]{3,2,1,0:T(8,128)(2,1)S(1)} %get-tuple-element.171), channel_id=1, source_target_pairs={{0,1},{2,3},{4,5},{6,7},{8,9},{10,11},{12,13},{14,15},{16,17},{18,... | collective-permute-start | bytes 430088 | tf_op jit(solution)/shard_map/ppermute | solution.py:15
  120.2 15.5 %copy-start.30 = (f32[3,3,2240]{2,1,0:T(4,128)S(1)}, f32[3,3,2240]{2,1,0:T(4,128)}, u32[]{:S(2)}) copy-start(f32[3,3,2240]{2,1,0:T(4,128)} %param.13) | copy-start | bytes 241924
  121.1 107.4 %all-gather.15.cloned.1.call-start = ((), (), s32[]{:S(2)}) async-start(), calls=%async_computation.5 | async-start | bytes 2580480 | tf_op jit(solution)/shard_map/all_gather | solution.py:41
  130.7 5.8 %collective-permute-start.3 = (bf16[1,1,32,2240]{3,2,1,0:T(8,128)(2,1)S(1)}, bf16[1,1,32,2240]{3,2,1,0:T(8,128)(2,1)S(1)}, u32[]{:S(2)}, u32[]{:S(2)}) collective-permute-start(bf16[1,1,32,2240]{3,2,1,0:T(8,128)(2,1)S(1)} %get-tuple-element.170), channel_id=1, source_target_pairs={{1,0},{3,2},{5,4},{7,6},{9,8},{11,10},{13,12},{15,14},{17,16},{19,... | collective-permute-start | bytes 430088 | tf_op jit(solution)/shard_map/ppermute | solution.py:18
  132.0 5.2 %collective-permute-start.2 = (bf16[1,1,32,2240]{3,2,1,0:T(8,128)(2,1)S(1)}, bf16[1,1,32,2240]{3,2,1,0:T(8,128)(2,1)}, u32[]{:S(2)}, u32[]{:S(2)}) collective-permute-start(bf16[1,1,32,2240]{3,2,1,0:T(8,128)(2,1)S(1)} %get-tuple-element.169), channel_id=1, source_target_pairs={{0,1},{2,3},{4,5},{6,7},{8,9},{10,11},{12,13},{14,15},{16,17},{18,... | collective-permute-start | bytes 430088 | tf_op jit(solution)/shard_map/ppermute | solution.py:15
  171.4 4.1 %copy-start.37 = (f32[128,20]{0,1:T(8,128)S(1)}, f32[128,20]{0,1:T(8,128)}, u32[]{:S(2)}) copy-start(f32[128,20]{0,1:T(8,128)} %copy-done.36) | copy-start | bytes 30724
  181.1 9.4 %copy-start.21 = (f32[2240]{0:T(1024)S(1)}, f32[2240]{0:T(1024)}, u32[]{:S(2)}) copy-start(f32[2240]{0:T(1024)} %get-tuple-element.137) | copy-start | bytes 26884
  188.3 5.6 %copy-start.31 = (f32[16,112]{1,0:T(8,128)}, f32[16,112]{1,0:T(8,128)S(1)}, u32[]{:S(2)}) copy-start(f32[16,112]{1,0:T(8,128)S(1)} %fusion.1) | copy-start | bytes 21508
  188.3 8.9 %collective-permute-start.5 = (f32[6,112]{1,0:T(8,128)S(1)}, f32[6,112]{1,0:T(8,128)S(1)}, u32[]{:S(2)}, u32[]{:S(2)}) collective-permute-start(f32[6,112]{1,0:T(8,128)S(1)} %slice.159), channel_id=1, source_target_pairs={{0,1},{2,3},{4,5},{6,7},{8,9},{10,11},{12,13},{14,15},{16,17},{18,... | collective-permute-start | bytes 8072
  190.5 3.4 %copy-start.16 = (f32[20,112,112]{2,1,0:T(8,128)S(1)}, f32[20,112,112]{2,1,0:T(8,128)}, u32[]{:S(2)}) copy-start(f32[20,112,112]{2,1,0:T(8,128)} %copy-done.15) | copy-start | bytes 3010564
  228.5 7.8 %copy-start.13 = (f32[10,112,112]{2,1,0:T(8,128)S(1)}, f32[10,112,112]{2,1,0:T(8,128)}, u32[]{:S(2)}) copy-start(f32[10,112,112]{2,1,0:T(8,128)} %reduce-scatter.9.cloned.1.call-done) | copy-start | bytes 1505284
  236.4 4.4 %copy-start.6 = (bf16[128,20,112]{0,2,1:T(8,128)(2,1)S(1)}, bf16[128,20,112]{0,2,1:T(8,128)(2,1)}, u32[]{:S(2)}) copy-start(bf16[128,20,112]{0,2,1:T(8,128)(2,1)} %copy-done.5) | copy-start | bytes 1720324
  (27 other events, 66.6 us)
Sparse Core Ops, SparseCore 0:
  14.2 11.1 reduce-scatter.6
  27.6 79.4 all-gather.12
  113.4 15.3 reduce-scatter.8
Sparse Core Ops, SparseCore 1:
  121.2 47.2 all-gather.16
  170.5 50.2 all-gather.14
